TPU v7x, 512 devices: a whole 4x8x8 slice. The times are simulated.
512 devices in a mesh: dp: 64 (over z, y_hi, x), shard: 8 (over y_lo, core).
Axes of the slice: x: 4, y: 8 (y_hi: 2, y_lo: 4; y = y_hi * 4 + y_lo), z: 8, core: 2. Of those that a mesh axis runs over, the one named last changes fastest.
Arguments:
- inputs: bfloat16 [512, 8, 8, 8, 256], P(('dp', 'shard')), may hold values from -24 to 24
- cotangent: bfloat16 [512, 4, 4, 4, 256], P(('dp', 'shard')), may hold values from -6 to 6
- weights: bfloat16 [28, 256, 256], P(None, 'shard'), may hold values from -0.078125 to 0.078125
Outputs:
- outputs: bfloat16 [512, 4, 4, 4, 256], P(('dp', 'shard'))
- input_grad: bfloat16 [512, 8, 8, 8, 256], P(('dp', 'shard'))
- weight_grad: float32 [28, 256, 256], P(None, 'shard')
All inputs are finite; a program needn't handle non-finite values.
Results may differ from a plain program's by a relative error of at most 0.012.
Values may be sent and summed in bfloat16 or wider, within the bound.
A program may use at most 64 MiB of HBM per device.

v0:
```python
import jax
import jax.numpy as jnp
from jax import lax
from jax.sharding import PartitionSpec as P


def build_cols(values):
    edge = values.shape[0]
    half = edge // 2
    width = values.shape[3]
    act = jax.nn.silu(values.astype(jnp.float32)).astype(jnp.bfloat16)
    padded = jnp.pad(act, ((1, 1), (1, 1), (1, 1), (0, 0)))
    pieces = []
    for first in range(3):
        for second in range(3):
            for third in range(3):
                pieces.append(
                    padded[
                        first : first + edge : 2,
                        second : second + edge : 2,
                        third : third + edge : 2,
                    ]
                )
    pieces.append(values[0::2, 0::2, 0::2])
    return jnp.stack(pieces, axis=3).reshape(half * half * half, 28, width)


def spread_back(values, grad_rows, piece, half):
    width = piece.shape[1]
    edge = 2 * half
    grid = jnp.zeros((edge + 2, edge + 2, edge + 2, width), jnp.float32)
    for first in range(3):
        block = jnp.einsum(
            "qo,tco->qtc",
            grad_rows,
            piece[9 * first : 9 * first + 9],
            preferred_element_type=jnp.float32,
        )
        block = block.reshape(half, half, half, 9, width)
        for second in range(3):
            for third in range(3):
                grid = grid.at[
                    first : first + edge : 2, second : second + edge : 2, third : third + edge : 2
                ].add(block[:, :, :, 3 * second + third])
    direct = jnp.einsum(
        "qo,co->qc", grad_rows, piece[27], preferred_element_type=jnp.float32
    ).reshape(half, half, half, width)
    own = values.astype(jnp.float32)
    sigma = jax.nn.sigmoid(own)
    grad_in = grid[1:-1, 1:-1, 1:-1] * sigma * (1.0 + own * (1.0 - sigma))
    grad_in = grad_in.at[0::2, 0::2, 0::2].add(direct)
    return grad_in.astype(jnp.bfloat16)


def shards(inputs, cotangent, weights):
    values = inputs[0]
    edge = values.shape[0]
    half = edge // 2
    chans = values.shape[3]
    taps_count = weights.shape[0]
    cols = build_cols(values)
    grad_rows = cotangent[0].reshape(half * half * half, chans)
    result = jnp.einsum(
        "qtc,tco->qo",
        cols,
        lax.all_gather(weights, "shard", axis=1, tiled=True),
        preferred_element_type=jnp.float32,
    )
    grad_in = spread_back(
        values, grad_rows, lax.all_gather(weights, "shard", axis=1, tiled=True), half
    )
    term = lax.dot_general(
        cols.reshape(half * half * half, taps_count * chans),
        grad_rows,
        (((0,), (0,)), ((), ())),
        preferred_element_type=jnp.float32,
    )
    term = term.astype(jnp.bfloat16).astype(jnp.float32).reshape(taps_count, chans, chans)
    owned = lax.psum_scatter(
        term.astype(jnp.bfloat16), "shard", scatter_dimension=1, tiled=True
    ).astype(jnp.float32)
    weight_grad = lax.psum(owned, "dp")
    outputs = result.astype(jnp.bfloat16).reshape(1, half, half, half, chans)
    return (outputs, grad_in.reshape(1, edge, edge, edge, chans), weight_grad)


def solution(mesh):
    return jax.shard_map(
        shards,
        mesh=mesh,
        in_specs=(
            P(("dp", "shard"), None, None, None, None),
            P(("dp", "shard"), None, None, None, None),
            P(None, "shard", None),
        ),
        out_specs=(
            P(("dp", "shard"), None, None, None, None),
            P(("dp", "shard"), None, None, None, None),
            P(None, "shard", None),
        ),
        check_vma=False,
    )
```

profile of v0, /device:TPU:8, one launch (start us, length us, event | category | flops | bytes accessed | tf_op | source)
XLA Modules:
  0.0 727.1 jit_solution(8520491467379494696)
XLA Ops:
  10.8 5.8 slice.207
  17.4 45.1 %all-gather.2.cloned.1.call-done = bf16[28,256,256]{2,1,0:T(8,128)(2,1)} async-done(((bf16[28,32,256]{2,1,0:T(8,128)(2,1)}), bf16[28,256,256]{2,1,0:T(8,128)(2,1)}) %all-gather.2.cloned.1.call-update) | async-done | bytes 3670032 | tf_op jit(solution)/shard_map/all_gather | solution.py:66
  70.1 5.2 scatter_fusion
  75.3 4.8 scatter_fusion.1
  84.9 4.8 scatter_fusion.3
  89.7 4.8 scatter_fusion.4
  99.3 4.8 scatter_fusion.6
  104.2 4.8 scatter_fusion.7
  113.8 5.0 scatter_fusion.9
  118.7 4.8 scatter_fusion.10
  123.6 4.8 scatter_fusion.11
  128.3 4.8 scatter_fusion.12
  133.2 4.8 scatter_fusion.13
  142.8 4.8 scatter_fusion.15
  147.6 4.8 scatter_fusion.16
  157.2 4.8 scatter_fusion.18
  162.0 4.8 scatter_fusion.19
  166.8 5.0 scatter_fusion.20
  171.8 4.8 scatter_fusion.21
  176.6 4.8 scatter_fusion.22
  186.2 4.8 scatter_fusion.24
  191.0 4.8 scatter_fusion.25
  228.6 41.0 %reduce-scatter.2.cloned.1.call-done = bf16[28,32,256]{2,1,0:T(8,128)(2,1)} async-done(((bf16[28,256,256]{2,1,0:T(8,128)(2,1)}), bf16[28,32,256]{2,1,0:T(8,128)(2,1)}) %reduce-scatter.2.cloned.1.call-update) | async-done | bytes 458768 | tf_op jit(solution)/shard_map/reduce_scatter | solution.py:79
  269.6 450.2 %all-reduce.2 = f32[28,32,256]{2,1,0:T(8,128)} all-reduce(bf16[28,32,256]{2,1,0:T(8,128)(2,1)} %reduce-scatter.2.cloned.1.call-done), channel_id=1, replica_groups=mesh['dp'=64,'shard'=8] {'dp'}, use_global_device_ids=true, to_apply=%region_29.30 | all-reduce | flops 229376 | bytes 1376256 | tf_op jit(solution)/shard_map/psum | solution.py:82
  (212 shorter events, 72.1 us)
Async XLA Ops:
  7.2 55.4 %all-gather.2.cloned.1.call-start = ((), (), s32[]{:S(2)}) async-start(), calls=%async_computation.1 | async-start | bytes 4128768 | tf_op jit(solution)/shard_map/all_gather | solution.py:66
  7.9 261.7 %reduce-scatter.2.cloned.1.call-start = ((), (), s32[]{:S(2)}) async-start(), calls=%async_computation.2 | async-start | bytes 4128768 | tf_op jit(solution)/shard_map/reduce_scatter | solution.py:79
  64.3 1.1 copy-start
  186.2 14.4 %copy-start.1 = (bf16[1,8,8,8,256]{4,3,2,1,0:T(8,128)(2,1)S(1)}, bf16[1,8,8,8,256]{4,3,2,1,0:T(8,128)(2,1)}, u32[]{:S(2)}) copy-start(bf16[1,8,8,8,256]{4,3,2,1,0:T(8,128)(2,1)} %param.3) | copy-start | bytes 786436
Sparse Core Ops, SparseCore 0:
  10.1 52.4 all-gather.1
  217.7 51.9 reduce-scatter.1
where the time goes:
time: 737 us; the launch traced here: 727 us
  blocking collectives  450 us (61%)
  other arithmetic  136 us (18%)
  waiting for transfers between devices  86.9 us (12%)
  local copies, waits for them, and re-layouts  25.6 us (3%)
  between operations  15.9 us (2%)
  matrix products  12.2 us (2%)
    psum x1, blocking collectives, shards(): weight_grad = lax.psum(owned, 'dp')  450 us
    scatter-add x27, other arithmetic, spread_back(): grid = grid.at[first:first + edge:2, second:second + edge:2, third:third...  130 us
    all_gather x1, waiting for transfers between devices, shards(): lax.all_gather(weights, 'shard', axis=1, tiled=True)  45.1 us
    reduce_scatter x1, waiting for transfers between devices, shards(): lax.psum_scatter(term.astype(jnp.bfloat16), 'shard', scatter_dimension=1,...  41 us
  transfers between devices with their start and end apart: 2, of which 2 were waited for; matrix products, arithmetic and copies ran while one was open for 3% of the time, Pallas kernels for 0%

commit v1 on v0

v1 whole, which is shorter than its diff:
```python
import functools

import jax
import jax.numpy as jnp
from jax import lax
from jax.experimental import pallas as pl
from jax.experimental.pallas import tpu as pltpu
from jax.sharding import PartitionSpec as P

F32 = jnp.float32
BF16 = jnp.bfloat16
MESH = pl.DeviceIdType.MESH

COMBOS = [(si, sj, sk) for si in (0, -1) for sj in (0, -1) for sk in (0, -1)]
DIRECT = 2


def lane_of(combo):
    return (256 * combo, 256) if combo < 4 else (1024 + 128 * (combo - 4), 128)


def tap_of(combo, parity):
    total = 0
    for weight, shift, odd in zip((9, 3, 1), COMBOS[combo], parity):
        if shift and not odd:
            return None
        total += weight * (1 if not odd else 0 if shift else 2)
    return total


PARITIES = [(a, b, c) for a in (0, 1) for b in (0, 1) for c in (0, 1)]


def dot(a, b, dims):
    return lax.dot_general(a, b, (dims, ((), ())), preferred_element_type=F32)


NN = ((1,), (0,))
NT = ((1,), (1,))
TN = ((0,), (0,))


def one_hot(hit):
    return jnp.where(hit, 1.0, 0.0).astype(BF16)


def sort_target(rows):
    k, j, i = rows & 3, (rows >> 2) & 3, (rows >> 4) & 1
    pk, pj, pi = (rows >> 5) & 1, (rows >> 6) & 1, (rows >> 7) & 1
    return (2 * i + pi) * 64 + (2 * j + pj) * 8 + 2 * k + pk


def kernel(nx, nz, x_hbm, g_hbm, w_hbm, out_hbm, ig_hbm, wg_hbm,
           x_in, g_in, w_in, sortm, sortmt, shiftm, shiftmt, sorted_x, send_x,
           recv_x, recv_g, cols, gcols, wf, wcat, w27, dsilu, gact, send_o, recv_o, own_o,
           send_i, recv_i, out_v, ig_v, gsend, g1, s2, r2, fin,
           in_sem, out_sem, xs, xr, gs, gr, os_, or_, is_, ir, s1s, s1r, s2s, s2r,
           s3s, s3r, s4s, s4r):
    nq = 2 * nz
    taps_x = 28 // nx
    rows_x = taps_x * 32
    rows_q = s2.shape[1]
    dp = lax.axis_index("dp")
    shard = lax.axis_index("shard")
    px = lax.rem(dp, nx)
    y_hi = lax.rem(lax.div(dp, nx), 2)
    pz = lax.div(dp, 2 * nx)
    y = y_hi * 4 + lax.div(shard, 2)
    core = lax.rem(shard, 2)
    sign = 1 - 2 * core
    q = pz * 2 + y_hi

    def at(pz_, y_, px_, core_):
        y_ = lax.rem(y_ + 8, 8)
        return ((pz_ * 2 + lax.div(y_, 4)) * nx + px_, lax.rem(y_, 4) * 2 + core_)

    def slice_of(y_, core_):
        return lax.rem(y_ + 8, 4) * 2 + core_

    def x_peer(d):
        return at(pz, y, lax.rem(px + d, nx), core)

    def q_peer(d):
        other = lax.rem(q + d, nq)
        return at(lax.div(other, 2), lax.rem(other, 2) * 4 + lax.rem(y, 4), px, core)

    def copy(src, dst, send, recv, dev):
        return pltpu.make_async_remote_copy(
            src_ref=src, dst_ref=dst, send_sem=send, recv_sem=recv, device_id=dev, device_id_type=MESH)

    loads = [pltpu.make_async_copy(a, b, in_sem.at[n]) for n, (a, b) in enumerate(((x_hbm, x_in), (g_hbm, g_in), (w_hbm, w_in)))]
    for load in loads:
        load.start()

    peers = [at(pz, y, px, 1 - core)]
    for d in (1, -1):
        for c in (0, 1):
            peers.append(at(pz, y + d, px, c))
    peers += [at(pz, y + 2 * sign, px, core), at(pz, y + 2 * sign, px, 1 - core), at(pz, y - 2 * sign, px, core)]
    peers += [x_peer(d) for d in range(1, nx)]
    peers += [q_peer(d) for d in range(1, nq)]
    barrier = pltpu.get_barrier_semaphore()
    for peer in peers:
        pl.semaphore_signal(barrier, inc=1, device_id=peer, device_id_type=MESH)

    row = lax.broadcasted_iota(jnp.int32, (256, 256), 0)
    col = lax.broadcasted_iota(jnp.int32, (256, 256), 1)
    sortm[...] = one_hot(sort_target(row) == col)
    loads[0].wait()
    for b in range(2):
        got = dot(sortm[...], x_in[b * 256:b * 256 + 256, :], NN)
        for par in range(8):
            sorted_x[par, b * 32:b * 32 + 32, :] = got[par * 32:par * 32 + 32, :]
    for p in range(8):
        for h in range(2):
            send_x[p, :, h * 128:h * 128 + 128] = jnp.concatenate(
                [sorted_x[4 * h + n, :, p * 32:p * 32 + 32] for n in range(4)], axis=1).astype(BF16)
    loads[1].wait()
    pl.semaphore_wait(barrier, len(peers))

    def far(c):
        return 2 - 4 * c

    def to_chip(k):
        return (y, y + 1, y - 1, y + 2 * sign)[k]

    sends = []
    for k in (3, 1, 2, 0):
        for e in (0, 1):
            if k == 0 and e == 0:
                continue
            c = lax.rem(core + e, 2)
            n = 2 * k + e
            dev = at(pz, to_chip(k), px, c)
            slot = 2 * k + core
            sends.append(copy(send_x.at[slice_of(to_chip(k), c)], recv_x.at[slot], xs.at[n], xr.at[slot], dev))
            sends.append(copy(g_in, recv_g.at[slot], gs.at[n], gr.at[slot], dev))
    for send in sends:
        send.start()
    recv_x[core] = send_x[shard]
    recv_g[core] = g_in[...]

    sortmt[...] = one_hot(sort_target(col) == row)
    ri, rj, rk = (row >> 4) & 3, (row >> 2) & 3, row & 3
    ci, cj, ck = (col >> 4) & 3, (col >> 2) & 3, col & 3
    for n, (si, sj, sk) in enumerate(COMBOS):
        if n == 0:
            continue
        step = 16 * si + 4 * sj + sk
        ok = (col == row + step) & (ri >= -si) & (rj >= -sj) & (rk >= -sk)
        shiftm[n] = one_hot(ok)
        ok = (row == col + step) & (ci >= -si) & (cj >= -sj) & (ck >= -sk)
        shiftmt[n] = one_hot(ok)
    wf[...] = jnp.zeros_like(wf)
    wcat[...] = jnp.zeros_like(wcat)
    w27[...] = jnp.zeros_like(w27)
    loads[2].wait()
    for n in range(8):
        first, width = lane_of(n)
        for par, parity in enumerate(PARITIES):
            tap = tap_of(n, parity)
            if tap is None:
                continue
            at_row = first + par * 32 - (256 - width)
            wf[at_row:at_row + 32, :] = w_in[tap]
            wcat[par * 32:par * 32 + 32, n * 256:n * 256 + 256] = w_in[tap]
    first = lane_of(DIRECT)[0]
    wf[first:first + 32, :] = w_in[27]
    w27[0:32, :] = w_in[27]

    def arrived(k, s):
        slot = 2 * k + s
        for buf, sem in ((recv_x, xr), (recv_g, gr)):
            copy(buf.at[slot], buf.at[slot], xs.at[0], sem.at[slot], at(pz, y, px, 1 - core)).wait_recv()

    for half in range(2):
        rows = slice(half * 256, half * 256 + 256)
        if half == 0:
            arrived(0, 1 - core)
            arrived(1, 0)
            arrived(1, 1)
        else:
            for k in (2, 3):
                arrived(k, 0)
                arrived(k, 1)
        raw = recv_x[4 * half:4 * half + 4].reshape(256, 256)
        v = raw.astype(F32)
        s = 1.0 / (1.0 + jnp.exp(-v))
        act = (v * s).astype(BF16)
        dsilu[rows, :] = s * (1.0 + v * (1.0 - s))
        cols[rows, 0:256] = act
        lane = lax.broadcasted_iota(jnp.int32, (256, 256), 1)
        for n in range(1, 8):
            first, width = lane_of(n)
            moved = dot(shiftm[n], act[:, 256 - width:], NN)
            if n == DIRECT:
                moved = jnp.where(lane < 32, v, moved)
            cols[rows, first:first + width] = moved.astype(BF16)

    grads = recv_g[...].reshape(512, 256)
    for block in range(6):
        got = dot(cols[:, block * 256:block * 256 + 256], grads, TN).astype(BF16)
        for n in range(8):
            first, width = lane_of(n)
            if first // 256 != block:
                continue
            for par, parity in enumerate(PARITIES):
                tap = tap_of(n, parity)
                if n == DIRECT and par == 0:
                    tap = 27
                if tap is None:
                    continue
                start = first + par * 32 - (256 - width) - block * 256
                place = (tap % taps_x) * 32
                gsend[tap // taps_x, place:place + 32, :] = got[start:start + 32, :]
    step1 = []
    for d in range(1, nx):
        other = lax.rem(px + d, nx)
        step1.append(copy(gsend.at[other], g1.at[d - 1], s1s.at[d - 1], s1r.at[d - 1], x_peer(d)))
    for send in step1:
        send.start()

    gcols[:, 0:256] = grads
    for half in range(2):
        rows = slice(half * 256, half * 256 + 256)
        for n in range(1, 8):
            gcols[rows, n * 256:n * 256 + 256] = dot(shiftmt[n], grads[rows, :], NN).astype(BF16)
    for half in range(2):
        rows = slice(half * 256, half * 256 + 256)
        got = dot(gcols[rows, :], wcat[...], NT) * dsilu[rows, :]
        direct = dot(grads[rows, :], w27[...], NT)
        for n in range(4):
            one = got[n * 64:n * 64 + 64, :]
            slot = 4 * half + n
            send_i[slot, :, 0:128] = (one[:, 0:128] + direct[n * 64:n * 64 + 64, :]).astype(BF16)
            send_i[slot, :, 128:256] = one[:, 128:256].astype(BF16)
        got = dot(cols[rows, :], wf[...], NN)
        gact[rows, :] = got
        for n in range(4):
            send_o[4 * half + n] = got[n * 64:n * 64 + 64, :].astype(BF16)
    home = []
    for k in (3, 1, 2, 0):
        for e in (0, 1):
            if k == 0 and e == 0:
                continue
            s = e if k else 1 - core
            chip = (y, y - 1, y + 1, y - far(e))[k]
            slot = 2 * k + s
            dev = at(pz, chip, px, s)
            n = 2 * k + e
            home.append(copy(send_i.at[slot], recv_i.at[shard], is_.at[n], ir.at[shard], dev))
            home.append(copy(send_o.at[slot], recv_o.at[shard], os_.at[n], or_.at[shard], dev))
    for send in home:
        send.start()
    recv_i[shard] = send_i[core]
    recv_o[shard] = send_o[core]

    for d in range(1, nx):
        step1[d - 1].wait()
    total = gsend[px].astype(F32)
    for d in range(1, nx):
        total = total + g1[d - 1].astype(F32)
    flat = s2.shape[0] * rows_q
    padded = total.astype(BF16)
    if flat > rows_x:
        padded = jnp.concatenate([padded, jnp.zeros((flat - rows_x, 256), BF16)], axis=0)
    for n in range(nq):
        s2[n] = padded[n * rows_q:n * rows_q + rows_q, :]
    step2 = []
    for d in range(1, nq):
        other = lax.rem(q + d, nq)
        step2.append(copy(s2.at[other], r2.at[d - 1], s2s.at[d - 1], s2r.at[d - 1], q_peer(d)))
    for send in step2:
        send.start()

    for e in range(1, 8):
        slot = lax.rem(shard + e, 8)
        for buf, ssem, sem in ((recv_i, is_, ir), (recv_o, os_, or_)):
            copy(buf.at[slot], buf.at[slot], ssem.at[0], sem.at[slot], at(pz, y, px, 1 - core)).wait_recv()
    out_v[...] = jnp.sum(recv_o[...].astype(F32), axis=0).astype(BF16)
    for par in range(8):
        for h in range(2):
            sorted_x[par, :, h * 128:h * 128 + 128] = jnp.concatenate(
                [recv_i[4 * h + n, :, par * 32:par * 32 + 32].astype(F32) for n in range(4)], axis=1)
    for b in range(2):
        natural = sorted_x[:, b * 32:b * 32 + 32, :].reshape(256, 256).astype(BF16)
        ig_v[b * 256:b * 256 + 256, :] = dot(sortmt[...], natural, NN).astype(BF16)
    stores = [pltpu.make_async_copy(out_v, out_hbm, out_sem.at[0]), pltpu.make_async_copy(ig_v, ig_hbm, out_sem.at[1])]
    for store in stores:
        store.start()

    for send in step2:
        send.wait()
    chunk = s2[q].astype(F32)
    for d in range(1, nq):
        chunk = chunk + r2[d - 1].astype(F32)
    mine = pl.ds(pl.multiple_of(q * rows_q, 16), rows_q)
    fin[px, mine, :] = chunk.astype(BF16)

    step3 = []
    for d in range(1, nq):
        step3.append(copy(fin.at[px, mine], fin.at[px, mine], s3s.at[d - 1], s3r.at[d - 1], q_peer(d)))
    for send in step3:
        send.start()
    for d in range(1, nq):
        other = lax.rem(q + nq - d, nq)
        theirs = pl.ds(pl.multiple_of(other * rows_q, 16), rows_q)
        copy(fin.at[px, theirs], fin.at[px, theirs], s3s.at[d - 1], s3r.at[d - 1], q_peer(d)).wait_recv()
    part = pl.ds(0, rows_x)
    step4 = []
    for d in range(1, nx):
        step4.append(copy(fin.at[px, part], fin.at[px, part], s4s.at[d - 1], s4r.at[d - 1], x_peer(d)))
    for send in step4:
        send.start()
    for d in range(1, nx):
        other = lax.rem(px + nx - d, nx)
        copy(fin.at[other, part], fin.at[other, part], s4s.at[d - 1], s4r.at[d - 1], x_peer(d)).wait_recv()
    last = pltpu.make_async_copy(fin.at[:, part], wg_hbm, out_sem.at[2])
    last.start()

    for send in sends + home + step3 + step4:
        send.wait_send()
    for store in stores:
        store.wait()
    last.wait()


def shards(nx, nz, inputs, cotangent, weights):
    nq = 2 * nz
    rows_x = 28 // nx * 32
    rows_q = -(-rows_x // nq // 16) * 16
    sems = [pltpu.SemaphoreType.DMA((n,)) for n in (3, 3, 8, 8, 8, 8, 8, 8, 8, 8)]
    sems += [pltpu.SemaphoreType.DMA((max(n - 1, 1),)) for n in (nx, nx, nq, nq, nq, nq, nx, nx)]
    vm = pltpu.VMEM
    scratch = [
        vm((512, 256), BF16), vm((64, 256), BF16), vm((28, 32, 256), BF16),
        vm((256, 256), BF16), vm((256, 256), BF16), vm((8, 256, 256), BF16), vm((8, 256, 256), BF16),
        vm((8, 64, 256), F32), vm((8, 64, 256), BF16),
        vm((8, 64, 256), BF16), vm((8, 64, 256), BF16),
        vm((512, 1536), BF16), vm((512, 2048), BF16),
        vm((1536, 256), BF16), vm((256, 2048), BF16), vm((128, 256), BF16),
        vm((512, 256), F32), vm((512, 256), F32),
        vm((8, 64, 256), BF16), vm((8, 64, 256), BF16), vm((64, 256), F32),
        vm((8, 64, 256), BF16), vm((8, 64, 256), BF16),
        vm((64, 256), BF16), vm((512, 256), BF16),
        vm((nx, rows_x, 256), BF16), vm((max(nx - 1, 1), rows_x, 256), BF16),
        vm((nq, rows_q, 256), BF16), vm((nq - 1, rows_q, 256), BF16),
        vm((nx, nq * rows_q, 256), BF16),
    ] + sems
    hbm = pl.BlockSpec(memory_space=pl.ANY)
    out, ig, wg = pl.pallas_call(
        functools.partial(kernel, nx, nz),
        out_shape=(
            jax.ShapeDtypeStruct((64, 256), BF16),
            jax.ShapeDtypeStruct((512, 256), BF16),
            jax.ShapeDtypeStruct((nx, rows_x, 256), BF16),
        ),
        in_specs=[hbm] * 3,
        out_specs=(hbm,) * 3,
        scratch_shapes=scratch,
        compiler_params=pltpu.CompilerParams(
            collective_id=0, has_side_effects=True, vmem_limit_bytes=48 * 2**20),
        name="unit",
    )(inputs.reshape(512, 256), cotangent.reshape(64, 256), weights)
    return (
        out.reshape(1, 4, 4, 4, 256),
        ig.reshape(1, 8, 8, 8, 256),
        wg.reshape(28, 32, 256).astype(F32),
    )


def solution(mesh, nx=4):
    nz = mesh.shape["dp"] // (2 * nx)
    rows = P(("dp", "shard"), None, None, None, None)
    return jax.shard_map(
        functools.partial(shards, nx, nz),
        mesh=mesh,
        in_specs=(rows, rows, P(None, "shard", None)),
        out_specs=(rows, rows, P(None, "shard", None)),
        check_vma=False,
    )
```

time: 737 us -> 61.8 us (0.08)
  the two profiles are of different devices: /device:TPU:8 before, /device:TPU:25 now
where the time goes in v1:
time: 61.8 us; the launch traced here: 61.5 us
  Pallas kernels  55.8 us (90%)
  local copies, waits for them, and re-layouts  4.07 us (7%)
  other arithmetic  1.02 us (2%)
  between operations  0.65 us (1%)
    pallas_call x1, Pallas kernels, shards(): pl.pallas_call(functools.partial(kernel, nx, nz), out_shape=(jax.ShapeDty...  55.8 us
    unnamed x5, local copies, waits for them, and re-layouts  2.66 us

profile of v1, /device:TPU:25, one launch (start us, length us, event | category | flops | bytes accessed | tf_op | source)
XLA Modules:
  0.0 61.5 jit_solution(11317634495345811363)
XLA Ops:
  0.6 0.8 %reshape.22.g_hbm = bf16[64,256]{1,0:T(8,128)(2,1)S(1)} reshape(bf16[1,4,4,4,256]{4,3,2,1,0:T(4,128)(2,1)} %param.4) | data formatting | bytes 65536 | tf_op jit(solution)/shard_map/reshape | solution.py:364
  1.4 0.0 copy-start
  1.4 1.0 %copy-done = bf16[28,32,256]{2,1,0:T(8,128)(2,1)S(1)} copy-done((bf16[28,32,256]{2,1,0:T(8,128)(2,1)S(1)}, bf16[28,32,256]{2,1,0:T(8,128)(2,1)}, u32[]{:S(2)}) %copy-start) | copy-done | bytes 458776
  2.4 0.0 copy-start.1
  2.4 0.9 %copy-done.1 = bf16[1,8,8,8,256]{4,3,2,1,0:T(8,128)(2,1)S(1)} copy-done((bf16[1,8,8,8,256]{4,3,2,1,0:T(8,128)(2,1)S(1)}, bf16[1,8,8,8,256]{4,3,2,1,0:T(8,128)(2,1)}, u32[]{:S(2)}) %copy-start.1) | copy-done | bytes 262168
  3.4 55.8 %unit.1 = (bf16[64,256]{1,0:T(8,128)(2,1)S(1)}, bf16[512,256]{1,0:T(8,128)(2,1)S(1)}, bf16[4,224,256]{2,1,0:T(8,128)(2,1)S(1)}) custom-call(bf16[512,256]{1,0:T(8,128)(2,1)S(1)} %bitcast.5, bf16[64,256]{1,0:T(8,128)(2,1)S(1)} %reshape.22.g_hbm, bf16[28,32,256]{2,1,0:T(8,128)(2,1)S(1)} %copy-done), custom_call_target="tpu_custom_call" | custom-call | tf_op jit(solution)/shard_map/unit/pallas_call | solution.py:351
  59.2 0.6 %reshape.23 = bf16[1,4,4,4,256]{4,3,2,1,0:T(4,128)(2,1)} reshape(bf16[64,256]{1,0:T(8,128)(2,1)S(1)} %get-tuple-element.6) | data formatting | bytes 65536 | tf_op jit(solution)/shard_map/reshape | solution.py:366
  59.8 1.0 %convert.1 = f32[28,32,256]{2,1,0:T(8,128)} convert(bf16[28,32,256]{2,1,0:T(8,128)(2,1)S(1)} %bitcast.4) | non-fusion elementwise | flops 229376 | bytes 1376256 | tf_op jit(solution)/shard_map/convert_element_type | solution.py:368
  60.8 0.7 %copy.7 = bf16[1,8,8,8,256]{4,3,2,1,0:T(8,128)(2,1)} copy(bf16[1,8,8,8,256]{4,3,2,1,0:T(8,128)(2,1)S(1)} %bitcast.6) | data formatting | bytes 524288
Async XLA Ops:
  1.4 1.0 %copy-start = (bf16[28,32,256]{2,1,0:T(8,128)(2,1)S(1)}, bf16[28,32,256]{2,1,0:T(8,128)(2,1)}, u32[]{:S(2)}) copy-start(bf16[28,32,256]{2,1,0:T(8,128)(2,1)} %w_hbm.1) | copy-start | bytes 1376260
  2.4 0.9 %copy-start.1 = (bf16[1,8,8,8,256]{4,3,2,1,0:T(8,128)(2,1)S(1)}, bf16[1,8,8,8,256]{4,3,2,1,0:T(8,128)(2,1)}, u32[]{:S(2)}) copy-start(bf16[1,8,8,8,256]{4,3,2,1,0:T(8,128)(2,1)} %param.3) | copy-start | bytes 786436

commit v2 on v1

--- a/solution.py
+++ b/solution.py
@@ -50,16 +50,18 @@
     return (2 * i + pi) * 64 + (2 * j + pj) * 8 + 2 * k + pk
 
 
-def kernel(nx, nz, x_hbm, g_hbm, w_hbm, out_hbm, ig_hbm, wg_hbm,
-           x_in, g_in, w_in, sortm, sortmt, shiftm, shiftmt, sorted_x, send_x,
-           recv_x, recv_g, cols, gcols, wf, wcat, w27, dsilu, gact, send_o, recv_o, own_o,
-           send_i, recv_i, out_v, ig_v, gsend, g1, s2, r2, fin,
-           in_sem, out_sem, xs, xr, gs, gr, os_, or_, is_, ir, s1s, s1r, s2s, s2r,
-           s3s, s3r, s4s, s4r):
+def kernel(nx, nz, x_hbm, g_hbm, w_hbm, out_v, ig_v, fin,
+           x_in, g_raw, g_in, w_in, sortm, sortmt, shiftm, shiftmt, sorted_x, send_x,
+           recv_x, recv_g, cols, gcols, wf, wcat, w27, dsilu, send_o, recv_o,
+           send_i, recv_i, gsend, g1, s2, r2,
+           in_sem, xs, xr, gs, gr, fs, os_, or_, is_, ir, s1s, s1r, s2s, s2r,
+           s3s, s3r, s4s, s4r, near, middle, across):
     nq = 2 * nz
+    quads = 2 if nz > 1 else 1
+    size = nz // quads
     taps_x = 28 // nx
-    rows_x = taps_x * 32
     rows_q = s2.shape[1]
+    rows_g = size * rows_q
     dp = lax.axis_index("dp")
     shard = lax.axis_index("shard")
     px = lax.rem(dp, nx)
@@ -68,7 +70,7 @@
     y = y_hi * 4 + lax.div(shard, 2)
     core = lax.rem(shard, 2)
     sign = 1 - 2 * core
-    q = pz * 2 + y_hi
+    q = y_hi * nz + pz
 
     def at(pz_, y_, px_, core_):
         y_ = lax.rem(y_ + 8, 8)
@@ -80,28 +82,36 @@
     def x_peer(d):
         return at(pz, y, lax.rem(px + d, nx), core)
 
-    def q_peer(d):
-        other = lax.rem(q + d, nq)
-        return at(lax.div(other, 2), lax.rem(other, 2) * 4 + lax.rem(y, 4), px, core)
+    def z_peer(d):
+        return at(lax.rem(pz + d + nz, nz), y, px, core)
+
+    def owner(other):
+        return at(lax.rem(other, nz), lax.div(other, nz) * 4 + lax.rem(y, 4), px, core)
+
+    partner = at(pz, y, px, 1 - core)
 
     def copy(src, dst, send, recv, dev):
         return pltpu.make_async_remote_copy(
             src_ref=src, dst_ref=dst, send_sem=send, recv_sem=recv, device_id=dev, device_id_type=MESH)
 
-    loads = [pltpu.make_async_copy(a, b, in_sem.at[n]) for n, (a, b) in enumerate(((x_hbm, x_in), (g_hbm, g_in), (w_hbm, w_in)))]
+    def signal(sem, dev):
+        pl.semaphore_signal(sem, inc=1, device_id=dev, device_id_type=MESH)
+
+    loads = [pltpu.make_async_copy(a, b, in_sem.at[n]) for n, (a, b) in enumerate(((x_hbm, x_in), (g_hbm, g_raw), (w_hbm, w_in)))]
     for load in loads:
         load.start()
 
-    peers = [at(pz, y, px, 1 - core)]
+    peers = [partner]
     for d in (1, -1):
         for c in (0, 1):
             peers.append(at(pz, y + d, px, c))
     peers += [at(pz, y + 2 * sign, px, core), at(pz, y + 2 * sign, px, 1 - core), at(pz, y - 2 * sign, px, core)]
     peers += [x_peer(d) for d in range(1, nx)]
-    peers += [q_peer(d) for d in range(1, nq)]
+    if nz > 1:
+        peers += [z_peer(1), z_peer(-1)]
     barrier = pltpu.get_barrier_semaphore()
     for peer in peers:
-        pl.semaphore_signal(barrier, inc=1, device_id=peer, device_id_type=MESH)
+        signal(barrier, peer)
 
     row = lax.broadcasted_iota(jnp.int32, (256, 256), 0)
     col = lax.broadcasted_iota(jnp.int32, (256, 256), 1)
@@ -116,6 +126,7 @@
             send_x[p, :, h * 128:h * 128 + 128] = jnp.concatenate(
                 [sorted_x[4 * h + n, :, p * 32:p * 32 + 32] for n in range(4)], axis=1).astype(BF16)
     loads[1].wait()
+    g_in[...] = g_raw[...].astype(F32).reshape(64, 256).astype(BF16)
     pl.semaphore_wait(barrier, len(peers))
 
     def far(c):
@@ -125,18 +136,23 @@
         return (y, y + 1, y - 1, y + 2 * sign)[k]
 
     sends = []
+    for k in (3, 1, 2):
+        slot = 2 * k + core
+        sends.append(copy(g_in, recv_g.at[slot], gs.at[k], gr.at[slot], at(pz, to_chip(k), px, core)))
+    sends.append(copy(g_in, recv_g.at[core], gs.at[0], gr.at[core], partner))
     for k in (3, 1, 2, 0):
         for e in (0, 1):
             if k == 0 and e == 0:
                 continue
             c = lax.rem(core + e, 2)
-            n = 2 * k + e
-            dev = at(pz, to_chip(k), px, c)
             slot = 2 * k + core
-            sends.append(copy(send_x.at[slice_of(to_chip(k), c)], recv_x.at[slot], xs.at[n], xr.at[slot], dev))
-            sends.append(copy(g_in, recv_g.at[slot], gs.at[n], gr.at[slot], dev))
+            sends.append(copy(send_x.at[slice_of(to_chip(k), c)], recv_x.at[slot], xs.at[2 * k + e], xr.at[slot],
+                              at(pz, to_chip(k), px, c)))
     for send in sends:
         send.start()
+    if nz > 1:
+        signal(near, z_peer(1))
+        signal(near, z_peer(-1))
     recv_x[core] = send_x[shard]
     recv_g[core] = g_in[...]
 
@@ -168,21 +184,26 @@
     wf[first:first + 32, :] = w_in[27]
     w27[0:32, :] = w_in[27]
 
-    def arrived(k, s):
-        slot = 2 * k + s
-        for buf, sem in ((recv_x, xr), (recv_g, gr)):
-            copy(buf.at[slot], buf.at[slot], xs.at[0], sem.at[slot], at(pz, y, px, 1 - core)).wait_recv()
+    if nz > 1:
+        pl.semaphore_wait(near, 2)
+        signal(middle, z_peer(2))
+        signal(middle, z_peer(-2))
+
+    def arrived(buf, sem, slot):
+        copy(buf.at[slot], buf.at[slot], xs.at[0], sem.at[slot], partner).wait_recv()
+
+    for k in (1, 2, 3):
+        slot = 2 * k + core
+        arrived(recv_g, gr, slot)
+        sends.append(copy(recv_g.at[slot], recv_g.at[slot], fs.at[k], gr.at[slot], partner))
+        sends[-1].start()
 
     for half in range(2):
         rows = slice(half * 256, half * 256 + 256)
-        if half == 0:
-            arrived(0, 1 - core)
-            arrived(1, 0)
-            arrived(1, 1)
-        else:
-            for k in (2, 3):
-                arrived(k, 0)
-                arrived(k, 1)
+        for k in (2 * half, 2 * half + 1):
+            for e in (0, 1):
+                if k or e:
+                    arrived(recv_x, xr, 2 * k + lax.rem(core + e, 2))
         raw = recv_x[4 * half:4 * half + 4].reshape(256, 256)
         v = raw.astype(F32)
         s = 1.0 / (1.0 + jnp.exp(-v))
@@ -197,6 +218,12 @@
                 moved = jnp.where(lane < 32, v, moved)
             cols[rows, first:first + width] = moved.astype(BF16)
 
+    for k in range(4):
+        arrived(recv_g, gr, 2 * k + 1 - core)
+    if nz > 1:
+        pl.semaphore_wait(middle, 2)
+    signal(across, at(pz, y + 4, px, core))
+
     grads = recv_g[...].reshape(512, 256)
     for block in range(6):
         got = dot(cols[:, block * 256:block * 256 + 256], grads, TN).astype(BF16)
@@ -213,10 +240,20 @@
                 start = first + par * 32 - (256 - width) - block * 256
                 place = (tap % taps_x) * 32
                 gsend[tap // taps_x, place:place + 32, :] = got[start:start + 32, :]
+    if rows_g * 2 * quads > taps_x * 32:
+        gsend[:, taps_x * 32:, :] = jnp.zeros((nx, rows_g * 2 * quads - taps_x * 32, 256), BF16)
+    zq = lax.div(pz, size)
+    groups = [(1 - y_hi) * quads + quads - 1 - zq, (1 - y_hi) * quads + zq, y_hi * quads + quads - 1 - zq, y_hi * quads + zq]
+    if quads == 1:
+        groups = groups[1::2]
+    ng = len(groups)
+    parts = [pl.ds(pl.multiple_of(g * rows_g, 16), rows_g) for g in groups]
     step1 = []
-    for d in range(1, nx):
-        other = lax.rem(px + d, nx)
-        step1.append(copy(gsend.at[other], g1.at[d - 1], s1s.at[d - 1], s1r.at[d - 1], x_peer(d)))
+    for r in range(ng):
+        for d in range(1, nx):
+            other = lax.rem(px + d, nx)
+            n = r * (nx - 1) + d - 1
+            step1.append(copy(gsend.at[other, parts[r]], g1.at[d - 1, r], s1s.at[n], s1r.at[n], x_peer(d)))
     for send in step1:
         send.start()
 
@@ -235,7 +272,6 @@
             send_i[slot, :, 0:128] = (one[:, 0:128] + direct[n * 64:n * 64 + 64, :]).astype(BF16)
             send_i[slot, :, 128:256] = one[:, 128:256].astype(BF16)
         got = dot(cols[rows, :], wf[...], NN)
-        gact[rows, :] = got
         for n in range(4):
             send_o[4 * half + n] = got[n * 64:n * 64 + 64, :].astype(BF16)
     home = []
@@ -255,23 +291,25 @@
     recv_i[shard] = send_i[core]
     recv_o[shard] = send_o[core]
 
-    for d in range(1, nx):
-        step1[d - 1].wait()
-    total = gsend[px].astype(F32)
-    for d in range(1, nx):
-        total = total + g1[d - 1].astype(F32)
-    flat = s2.shape[0] * rows_q
-    padded = total.astype(BF16)
-    if flat > rows_x:
-        padded = jnp.concatenate([padded, jnp.zeros((flat - rows_x, 256), BF16)], axis=0)
-    for n in range(nq):
-        s2[n] = padded[n * rows_q:n * rows_q + rows_q, :]
+    pl.semaphore_wait(across, 1)
     step2 = []
-    for d in range(1, nq):
-        other = lax.rem(q + d, nq)
-        step2.append(copy(s2.at[other], r2.at[d - 1], s2s.at[d - 1], s2r.at[d - 1], q_peer(d)))
-    for send in step2:
-        send.start()
+    for r in range(ng):
+        for d in range(1, nx):
+            step1[r * (nx - 1) + d - 1].wait()
+        total = gsend[px, parts[r], :].astype(F32)
+        for d in range(1, nx):
+            total = total + g1[d - 1, r].astype(F32)
+        total = total.astype(BF16)
+        for n in range(size):
+            s2[groups[r] * size + n] = total[n * rows_q:n * rows_q + rows_q, :]
+        for e in range(size - 1, -1, -1):
+            if r == ng - 1 and e == 0:
+                continue
+            other = groups[r] * size + lax.rem(pz + e, size)
+            n = r * size + e
+            step2.append(copy(s2.at[other], r2.at[q], s2s.at[n], s2r.at[q], owner(other)))
+            step2[-1].start()
+    r2[q] = s2[q]
 
     for e in range(1, 8):
         slot = lax.rem(shard + e, 8)
@@ -285,87 +323,116 @@
     for b in range(2):
         natural = sorted_x[:, b * 32:b * 32 + 32, :].reshape(256, 256).astype(BF16)
         ig_v[b * 256:b * 256 + 256, :] = dot(sortmt[...], natural, NN).astype(BF16)
-    stores = [pltpu.make_async_copy(out_v, out_hbm, out_sem.at[0]), pltpu.make_async_copy(ig_v, ig_hbm, out_sem.at[1])]
-    for store in stores:
-        store.start()
-
-    for send in step2:
-        send.wait()
-    chunk = s2[q].astype(F32)
+
     for d in range(1, nq):
-        chunk = chunk + r2[d - 1].astype(F32)
+        other = lax.rem(q + d, nq)
+        copy(r2.at[other], r2.at[other], s2s.at[0], s2r.at[other], partner).wait_recv()
     mine = pl.ds(pl.multiple_of(q * rows_q, 16), rows_q)
-    fin[px, mine, :] = chunk.astype(BF16)
+    fin[px, mine, :] = jnp.sum(r2[...].astype(F32), axis=0).astype(BF16)
 
     step3 = []
-    for d in range(1, nq):
-        step3.append(copy(fin.at[px, mine], fin.at[px, mine], s3s.at[d - 1], s3r.at[d - 1], q_peer(d)))
-    for send in step3:
-        send.start()
-    for d in range(1, nq):
-        other = lax.rem(q + nq - d, nq)
-        theirs = pl.ds(pl.multiple_of(other * rows_q, 16), rows_q)
-        copy(fin.at[px, theirs], fin.at[px, theirs], s3s.at[d - 1], s3r.at[d - 1], q_peer(d)).wait_recv()
-    part = pl.ds(0, rows_x)
+    for r in range(ng):
+        for e in range(size - 1, -1, -1):
+            if r == ng - 1 and e == 0:
+                continue
+            other = groups[r] * size + lax.rem(pz + e, size)
+            step3.append(copy(fin.at[px, mine], fin.at[px, mine], s3s.at[r * size + e], s3r.at[q], owner(other)))
+            step3[-1].start()
     step4 = []
-    for d in range(1, nx):
-        step4.append(copy(fin.at[px, part], fin.at[px, part], s4s.at[d - 1], s4r.at[d - 1], x_peer(d)))
-    for send in step4:
-        send.start()
-    for d in range(1, nx):
-        other = lax.rem(px + nx - d, nx)
-        copy(fin.at[other, part], fin.at[other, part], s4s.at[d - 1], s4r.at[d - 1], x_peer(d)).wait_recv()
-    last = pltpu.make_async_copy(fin.at[:, part], wg_hbm, out_sem.at[2])
-    last.start()
-
-    for send in sends + home + step3 + step4:
+    for r in range(ng - 1, -1, -1):
+        for e in range(size):
+            if r == ng - 1 and e == 0:
+                continue
+            other = groups[r] * size + lax.rem(pz + e, size)
+            theirs = pl.ds(pl.multiple_of(other * rows_q, 16), rows_q)
+            copy(fin.at[px, theirs], fin.at[px, theirs], s3s.at[0], s3r.at[other], partner).wait_recv()
+        for d in range(1, nx):
+            n = r * (nx - 1) + d - 1
+            step4.append(copy(fin.at[px, parts[r]], fin.at[px, parts[r]], s4s.at[n], s4r.at[n], x_peer(d)))
+            step4[-1].start()
+    for r in range(ng - 1, -1, -1):
+        for d in range(1, nx):
+            n = r * (nx - 1) + d - 1
+            other = lax.rem(px + nx - d, nx)
+            copy(fin.at[other, parts[r]], fin.at[other, parts[r]], s4s.at[n], s4r.at[n], x_peer(d)).wait_recv()
+    for send in sends + home + step2 + step3 + step4:
         send.wait_send()
+
+
+def finish(out_v, ig_v, fin, out_hbm, ig_hbm, wg_hbm, out_s, wg_s, sem):
+    nx, rows = wg_s.shape[:2]
+    stores = [pltpu.make_async_copy(ig_v, ig_hbm, sem.at[0])]
+    stores[0].start()
+    for n in range(nx):
+        wg_s[n] = fin[n, 0:rows, :].astype(F32)
+        stores.append(pltpu.make_async_copy(wg_s.at[n], wg_hbm.at[n], sem.at[n + 1]))
+        stores[-1].start()
+    out_s[...] = out_v[...].astype(F32).reshape(4, 4, 4, 256).astype(BF16)
+    stores.append(pltpu.make_async_copy(out_s, out_hbm, sem.at[nx + 1]))
+    stores[-1].start()
     for store in stores:
         store.wait()
-    last.wait()
 
 
 def shards(nx, nz, inputs, cotangent, weights):
     nq = 2 * nz
+    quads = 2 if nz > 1 else 1
+    ng = 2 * quads
     rows_x = 28 // nx * 32
     rows_q = -(-rows_x // nq // 16) * 16
-    sems = [pltpu.SemaphoreType.DMA((n,)) for n in (3, 3, 8, 8, 8, 8, 8, 8, 8, 8)]
-    sems += [pltpu.SemaphoreType.DMA((max(n - 1, 1),)) for n in (nx, nx, nq, nq, nq, nq, nx, nx)]
+    rows_g = nz // quads * rows_q
+    dma = pltpu.SemaphoreType.DMA
+    sems = [dma((n,)) for n in (3, 8, 8, 4, 8, 4, 8, 8, 8, 8)]
+    sems += [dma((max(n, 1),)) for n in (ng * (nx - 1), ng * (nx - 1), nq, nq, nq, nq, ng * (nx - 1), ng * (nx - 1))]
+    sems += [pltpu.SemaphoreType.REGULAR] * 3
     vm = pltpu.VMEM
     scratch = [
-        vm((512, 256), BF16), vm((64, 256), BF16), vm((28, 32, 256), BF16),
+        vm((512, 256), BF16), vm((4, 4, 4, 256), BF16), vm((64, 256), BF16), vm((28, 32, 256), BF16),
         vm((256, 256), BF16), vm((256, 256), BF16), vm((8, 256, 256), BF16), vm((8, 256, 256), BF16),
         vm((8, 64, 256), F32), vm((8, 64, 256), BF16),
         vm((8, 64, 256), BF16), vm((8, 64, 256), BF16),
         vm((512, 1536), BF16), vm((512, 2048), BF16),
         vm((1536, 256), BF16), vm((256, 2048), BF16), vm((128, 256), BF16),
-        vm((512, 256), F32), vm((512, 256), F32),
-        vm((8, 64, 256), BF16), vm((8, 64, 256), BF16), vm((64, 256), F32),
+        vm((512, 256), F32),
         vm((8, 64, 256), BF16), vm((8, 64, 256), BF16),
-        vm((64, 256), BF16), vm((512, 256), BF16),
-        vm((nx, rows_x, 256), BF16), vm((max(nx - 1, 1), rows_x, 256), BF16),
-        vm((nq, rows_q, 256), BF16), vm((nq - 1, rows_q, 256), BF16),
-        vm((nx, nq * rows_q, 256), BF16),
+        vm((8, 64, 256), BF16), vm((8, 64, 256), BF16),
+        vm((nx, ng * rows_g, 256), BF16), vm((max(nx - 1, 1), ng, rows_g, 256), BF16),
+        vm((nq, rows_q, 256), BF16), vm((nq, rows_q, 256), BF16),
     ] + sems
-    hbm = pl.BlockSpec(memory_space=pl.ANY)
+    hbm = pl.BlockSpec(memory_space=pltpu.HBM)
+    vmem = pl.BlockSpec(memory_space=pltpu.VMEM)
     out, ig, wg = pl.pallas_call(
         functools.partial(kernel, nx, nz),
         out_shape=(
             jax.ShapeDtypeStruct((64, 256), BF16),
             jax.ShapeDtypeStruct((512, 256), BF16),
-            jax.ShapeDtypeStruct((nx, rows_x, 256), BF16),
+            jax.ShapeDtypeStruct((nx, ng * rows_g, 256), BF16),
         ),
         in_specs=[hbm] * 3,
-        out_specs=(hbm,) * 3,
+        out_specs=(vmem,) * 3,
         scratch_shapes=scratch,
         compiler_params=pltpu.CompilerParams(
             collective_id=0, has_side_effects=True, vmem_limit_bytes=48 * 2**20),
         name="unit",
-    )(inputs.reshape(512, 256), cotangent.reshape(64, 256), weights)
+    )(*[pltpu.with_memory_space_constraint(a, pltpu.HBM)
+        for a in (inputs.reshape(512, 256), cotangent.reshape(4, 4, 4, 256), weights)])
+    out, ig, wg = pl.pallas_call(
+        finish,
+        out_shape=(
+            jax.ShapeDtypeStruct((4, 4, 4, 256), BF16),
+            jax.ShapeDtypeStruct((512, 256), BF16),
+            jax.ShapeDtypeStruct((nx, rows_x, 256), F32),
+        ),
+        in_specs=[vmem] * 3,
+        out_specs=(hbm,) * 3,
+        scratch_shapes=[vm((4, 4, 4, 256), BF16), vm((nx, rows_x, 256), F32), dma((nx + 2,))],
+        compiler_params=pltpu.CompilerParams(vmem_limit_bytes=8 * 2**20),
+        name="finish",
+    )(out, ig, wg)
     return (
         out.reshape(1, 4, 4, 4, 256),
         ig.reshape(1, 8, 8, 8, 256),
-        wg.reshape(28, 32, 256).astype(F32),
+        wg.reshape(28, 32, 256),
     )
 
 

time: 61.8 us -> 51.6 us (0.83)
  the two profiles are of different devices: /device:TPU:25 before, /device:TPU:1 now
where the time goes in v2:
time: 51.6 us; the launch traced here: 51.5 us
  Pallas kernels  50.8 us (98%)
  between operations  0.64 us (1%)
    pallas_call x1, Pallas kernels, shards(): pl.pallas_call(functools.partial(kernel, nx, nz), out_shape=(jax.ShapeDty...  49.8 us
    pallas_call x1, Pallas kernels, shards(): pl.pallas_call(finish, out_shape=(jax.ShapeDtypeStruct((4, 4, 4, 256), BF...  1.06 us

profile of v2, /device:TPU:1, one launch (start us, length us, event | category | flops | bytes accessed | tf_op | source)
XLA Modules:
  0.0 51.5 jit_solution(5843912834044278546)
XLA Ops:
  0.6 49.8 %unit.1 = (bf16[64,256]{1,0:T(8,128)(2,1)S(1)}, bf16[512,256]{1,0:T(8,128)(2,1)S(1)}, bf16[4,256,256]{2,1,0:T(8,128)(2,1)S(1)}) custom-call(bf16[512,256]{1,0:T(8,128)(2,1)} %bitcast.5, bf16[4,4,4,256]{3,2,1,0:T(4,128)(2,1)} %bitcast.6, bf16[28,32,256]{2,1,0:T(8,128)(2,1)} %w_hbm.1), custom_call_target="tpu_custom_call" | custom-call | tf_op jit(solution)/shard_map/unit/pallas_call | solution.py:404
  50.4 1.1 %finish.1 = (bf16[4,4,4,256]{3,2,1,0:T(4,128)(2,1)}, bf16[512,256]{1,0:T(8,128)(2,1)}, f32[4,224,256]{2,1,0:T(8,128)}) custom-call(bf16[64,256]{1,0:T(8,128)(2,1)S(1)} %get-tuple-element.9.out_v, bf16[512,256]{1,0:T(8,128)(2,1)S(1)} %get-tuple-element.10.ig_v, bf16[4,256,256]{2,1,0:T(8,128)(2,1)S(1)} %get-tuple-element.11.fin), custom_call_target="tpu_custom_call" | custom-call | tf_op jit(solution)/shard_map/finish/pallas_call | solution.py:419

commit v3 on v2

--- a/solution.py
+++ b/solution.py
@@ -12,6 +12,7 @@
 MESH = pl.DeviceIdType.MESH
 
 COMBOS = [(si, sj, sk) for si in (0, -1) for sj in (0, -1) for sk in (0, -1)]
+IDLE = 4
 DIRECT = 2
 
 
@@ -57,11 +58,9 @@
            in_sem, xs, xr, gs, gr, fs, os_, or_, is_, ir, s1s, s1r, s2s, s2r,
            s3s, s3r, s4s, s4r, near, middle, across):
     nq = 2 * nz
-    quads = 2 if nz > 1 else 1
-    size = nz // quads
     taps_x = 28 // nx
     rows_q = s2.shape[1]
-    rows_g = size * rows_q
+    ring = s2.shape[0] // 2
     dp = lax.axis_index("dp")
     shard = lax.axis_index("shard")
     px = lax.rem(dp, nx)
@@ -85,8 +84,22 @@
     def z_peer(d):
         return at(lax.rem(pz + d + nz, nz), y, px, core)
 
-    def owner(other):
-        return at(lax.rem(other, nz), lax.div(other, nz) * 4 + lax.rem(y, 4), px, core)
+    here = lax.rem(pz - lax.div(pz, IDLE + 1), nz) if ring < nz else pz
+    is_owner = pz != IDLE
+    mine = y_hi * ring + here
+
+    def owner(y_, n):
+        return at(n + lax.div(n, IDLE) if ring < nz else n, y_ * 4 + lax.rem(y, 4), px, core)
+
+    def order():
+        offsets = sorted(range(ring), key=lambda e: -min(e, ring - e))
+        for other_y in (1, 0):
+            for e in offsets:
+                y_ = 1 - y_hi if other_y else y_hi
+                yield not other_y and e == 0, y_, lax.rem(here + e, ring)
+
+    def piece(n):
+        return pl.ds(pl.multiple_of(n * rows_q, 16), rows_q)
 
     partner = at(pz, y, px, 1 - core)
 
@@ -148,11 +161,11 @@
             slot = 2 * k + core
             sends.append(copy(send_x.at[slice_of(to_chip(k), c)], recv_x.at[slot], xs.at[2 * k + e], xr.at[slot],
                               at(pz, to_chip(k), px, c)))
-    for send in sends:
-        send.start()
     if nz > 1:
         signal(near, z_peer(1))
         signal(near, z_peer(-1))
+    for send in sends:
+        send.start()
     recv_x[core] = send_x[shard]
     recv_g[core] = g_in[...]
 
@@ -184,11 +197,6 @@
     wf[first:first + 32, :] = w_in[27]
     w27[0:32, :] = w_in[27]
 
-    if nz > 1:
-        pl.semaphore_wait(near, 2)
-        signal(middle, z_peer(2))
-        signal(middle, z_peer(-2))
-
     def arrived(buf, sem, slot):
         copy(buf.at[slot], buf.at[slot], xs.at[0], sem.at[slot], partner).wait_recv()
 
@@ -200,6 +208,10 @@
 
     for half in range(2):
         rows = slice(half * 256, half * 256 + 256)
+        if nz > 1 and half == 1:
+            pl.semaphore_wait(near, 2)
+            signal(middle, z_peer(2))
+            signal(middle, z_peer(-2))
         for k in (2 * half, 2 * half + 1):
             for e in (0, 1):
                 if k or e:
@@ -240,22 +252,14 @@
                 start = first + par * 32 - (256 - width) - block * 256
                 place = (tap % taps_x) * 32
                 gsend[tap // taps_x, place:place + 32, :] = got[start:start + 32, :]
-    if rows_g * 2 * quads > taps_x * 32:
-        gsend[:, taps_x * 32:, :] = jnp.zeros((nx, rows_g * 2 * quads - taps_x * 32, 256), BF16)
-    zq = lax.div(pz, size)
-    groups = [(1 - y_hi) * quads + quads - 1 - zq, (1 - y_hi) * quads + zq, y_hi * quads + quads - 1 - zq, y_hi * quads + zq]
-    if quads == 1:
-        groups = groups[1::2]
-    ng = len(groups)
-    parts = [pl.ds(pl.multiple_of(g * rows_g, 16), rows_g) for g in groups]
     step1 = []
-    for r in range(ng):
+    for t, (_, y_, n) in enumerate(order()):
         for d in range(1, nx):
             other = lax.rem(px + d, nx)
-            n = r * (nx - 1) + d - 1
-            step1.append(copy(gsend.at[other, parts[r]], g1.at[d - 1, r], s1s.at[n], s1r.at[n], x_peer(d)))
-    for send in step1:
-        send.start()
+            m = t * (nx - 1) + d - 1
+            part = piece(y_ * ring + n)
+            step1.append(copy(gsend.at[other, part], g1.at[d - 1, t], s1s.at[m], s1r.at[m], x_peer(d)))
+            step1[-1].start()
 
     gcols[:, 0:256] = grads
     for half in range(2):
@@ -286,30 +290,67 @@
             n = 2 * k + e
             home.append(copy(send_i.at[slot], recv_i.at[shard], is_.at[n], ir.at[shard], dev))
             home.append(copy(send_o.at[slot], recv_o.at[shard], os_.at[n], or_.at[shard], dev))
+    pl.semaphore_wait(across, 1)
+    step2 = []
+    for t, (own, y_, n) in enumerate(order()):
+        for d in range(1, nx):
+            step1[t * (nx - 1) + d - 1].wait()
+        part = y_ * ring + n
+        total = gsend[px, piece(part), :].astype(F32)
+        for d in range(1, nx):
+            total = total + g1[d - 1, t].astype(F32)
+        s2[part] = total.astype(BF16)
+        send = copy(s2.at[part], r2.at[q], s2s.at[t], s2r.at[q], owner(y_, n))
+        if not own:
+            send.start()
+            step2.append(send)
+        elif ring < nz:
+            pl.when(pz == IDLE)(send.start)
+            last2 = send
+    r2[q] = s2[mine]
+
     for send in home:
         send.start()
     recv_i[shard] = send_i[core]
     recv_o[shard] = send_o[core]
 
-    pl.semaphore_wait(across, 1)
-    step2 = []
-    for r in range(ng):
+    def for_owners(body):
+        if ring < nz:
+            pl.when(is_owner)(body)
+        else:
+            body()
+
+    part = piece(mine)
+    step3 = [copy(fin.at[px, part], fin.at[px, part], s3s.at[t], s3r.at[q], owner(y_, n))
+             for t, (own, y_, n) in enumerate(order()) if not own]
+    if ring < nz:
+        for n, y_ in enumerate((1 - y_hi, y_hi)):
+            step3.append(copy(fin.at[px, part], fin.at[px, part], s3s.at[2 * ring + n], s3r.at[q],
+                              at(IDLE, y_ * 4 + lax.rem(y, 4), px, core)))
+
+    @for_owners
+    def _():
+        for d in range(1, nq):
+            other = lax.rem(q + d, nq)
+            copy(r2.at[other], r2.at[other], s2s.at[0], s2r.at[other], partner).wait_recv()
+        fin[px, part, :] = jnp.sum(r2[...].astype(F32), axis=0).astype(BF16)
+        for send in step3:
+            send.start()
+
+    step4 = []
+    places = list(order())[::-1]
+    for t, (own, y_, n) in enumerate(places):
+        theirs = piece(y_ * ring + n)
+        sender = y_ * nz + (n + lax.div(n, IDLE) if ring < nz else n)
+        come = copy(fin.at[px, theirs], fin.at[px, theirs], s3s.at[0], s3r.at[sender], partner)
+        if not own:
+            come.wait_recv()
+        elif ring < nz:
+            pl.when(pz == IDLE)(come.wait_recv)
         for d in range(1, nx):
-            step1[r * (nx - 1) + d - 1].wait()
-        total = gsend[px, parts[r], :].astype(F32)
-        for d in range(1, nx):
-            total = total + g1[d - 1, r].astype(F32)
-        total = total.astype(BF16)
-        for n in range(size):
-            s2[groups[r] * size + n] = total[n * rows_q:n * rows_q + rows_q, :]
-        for e in range(size - 1, -1, -1):
-            if r == ng - 1 and e == 0:
-                continue
-            other = groups[r] * size + lax.rem(pz + e, size)
-            n = r * size + e
-            step2.append(copy(s2.at[other], r2.at[q], s2s.at[n], s2r.at[q], owner(other)))
-            step2[-1].start()
-    r2[q] = s2[q]
+            m = t * (nx - 1) + d - 1
+            step4.append(copy(fin.at[px, theirs], fin.at[px, theirs], s4s.at[m], s4r.at[m], x_peer(d)))
+            step4[-1].start()
 
     for e in range(1, 8):
         slot = lax.rem(shard + e, 8)
@@ -324,39 +365,21 @@
         natural = sorted_x[:, b * 32:b * 32 + 32, :].reshape(256, 256).astype(BF16)
         ig_v[b * 256:b * 256 + 256, :] = dot(sortmt[...], natural, NN).astype(BF16)
 
-    for d in range(1, nq):
-        other = lax.rem(q + d, nq)
-        copy(r2.at[other], r2.at[other], s2s.at[0], s2r.at[other], partner).wait_recv()
-    mine = pl.ds(pl.multiple_of(q * rows_q, 16), rows_q)
-    fin[px, mine, :] = jnp.sum(r2[...].astype(F32), axis=0).astype(BF16)
-
-    step3 = []
-    for r in range(ng):
-        for e in range(size - 1, -1, -1):
-            if r == ng - 1 and e == 0:
-                continue
-            other = groups[r] * size + lax.rem(pz + e, size)
-            step3.append(copy(fin.at[px, mine], fin.at[px, mine], s3s.at[r * size + e], s3r.at[q], owner(other)))
-            step3[-1].start()
-    step4 = []
-    for r in range(ng - 1, -1, -1):
-        for e in range(size):
-            if r == ng - 1 and e == 0:
-                continue
-            other = groups[r] * size + lax.rem(pz + e, size)
-            theirs = pl.ds(pl.multiple_of(other * rows_q, 16), rows_q)
-            copy(fin.at[px, theirs], fin.at[px, theirs], s3s.at[0], s3r.at[other], partner).wait_recv()
+    for t, (own, y_, n) in enumerate(places):
+        theirs = piece(y_ * ring + n)
         for d in range(1, nx):
-            n = r * (nx - 1) + d - 1
-            step4.append(copy(fin.at[px, parts[r]], fin.at[px, parts[r]], s4s.at[n], s4r.at[n], x_peer(d)))
-            step4[-1].start()
-    for r in range(ng - 1, -1, -1):
-        for d in range(1, nx):
-            n = r * (nx - 1) + d - 1
+            m = t * (nx - 1) + d - 1
             other = lax.rem(px + nx - d, nx)
-            copy(fin.at[other, parts[r]], fin.at[other, parts[r]], s4s.at[n], s4r.at[n], x_peer(d)).wait_recv()
-    for send in sends + home + step2 + step3 + step4:
+            copy(fin.at[other, theirs], fin.at[other, theirs], s4s.at[m], s4r.at[m], x_peer(d)).wait_recv()
+    for send in sends + home + step2 + step4:
         send.wait_send()
+    if ring < nz:
+        pl.when(pz == IDLE)(last2.wait_send)
+
+    @for_owners
+    def _():
+        for send in step3:
+            send.wait_send()
 
 
 def finish(out_v, ig_v, fin, out_hbm, ig_hbm, wg_hbm, out_s, wg_s, sem):
@@ -376,14 +399,12 @@
 
 def shards(nx, nz, inputs, cotangent, weights):
     nq = 2 * nz
-    quads = 2 if nz > 1 else 1
-    ng = 2 * quads
+    owners = 14 if nz == 8 else nq
     rows_x = 28 // nx * 32
-    rows_q = -(-rows_x // nq // 16) * 16
-    rows_g = nz // quads * rows_q
+    rows_q = rows_x // owners
     dma = pltpu.SemaphoreType.DMA
     sems = [dma((n,)) for n in (3, 8, 8, 4, 8, 4, 8, 8, 8, 8)]
-    sems += [dma((max(n, 1),)) for n in (ng * (nx - 1), ng * (nx - 1), nq, nq, nq, nq, ng * (nx - 1), ng * (nx - 1))]
+    sems += [dma((max(n, 1),)) for n in (owners * (nx - 1), owners * (nx - 1), nq, nq, nq, nq, owners * (nx - 1), owners * (nx - 1))]
     sems += [pltpu.SemaphoreType.REGULAR] * 3
     vm = pltpu.VMEM
     scratch = [
@@ -396,8 +417,8 @@
         vm((512, 256), F32),
         vm((8, 64, 256), BF16), vm((8, 64, 256), BF16),
         vm((8, 64, 256), BF16), vm((8, 64, 256), BF16),
-        vm((nx, ng * rows_g, 256), BF16), vm((max(nx - 1, 1), ng, rows_g, 256), BF16),
-        vm((nq, rows_q, 256), BF16), vm((nq, rows_q, 256), BF16),
+        vm((nx, rows_x, 256), BF16), vm((max(nx - 1, 1), owners, rows_q, 256), BF16),
+        vm((owners, rows_q, 256), BF16), vm((nq, rows_q, 256), BF16),
     ] + sems
     hbm = pl.BlockSpec(memory_space=pltpu.HBM)
     vmem = pl.BlockSpec(memory_space=pltpu.VMEM)
@@ -406,7 +427,7 @@
         out_shape=(
             jax.ShapeDtypeStruct((64, 256), BF16),
             jax.ShapeDtypeStruct((512, 256), BF16),
-            jax.ShapeDtypeStruct((nx, ng * rows_g, 256), BF16),
+            jax.ShapeDtypeStruct((nx, rows_x, 256), BF16),
         ),
         in_specs=[hbm] * 3,
         out_specs=(vmem,) * 3,

time: 51.6 us -> 50.9 us (0.986)
  Pallas kernels: 50.8 us -> 50.1 us
    pallas_call x1, Pallas kernels: 49.8 us -> 49 us  [shards(): pl.pallas_call(functools.partial(kernel, nx, nz), out_shape=(jax.ShapeDty...]
where the time goes in v3:
time: 50.9 us; the launch traced here: 50.7 us
  Pallas kernels  50.1 us (98%)
  between operations  0.64 us (1%)
    pallas_call x1, Pallas kernels, shards(): pl.pallas_call(functools.partial(kernel, nx, nz), out_shape=(jax.ShapeDty...  49 us
    pallas_call x1, Pallas kernels, shards(): pl.pallas_call(finish, out_shape=(jax.ShapeDtypeStruct((4, 4, 4, 256), BF...  1.06 us

profile of v3, /device:TPU:1, one launch (start us, length us, event | category | flops | bytes accessed | tf_op | source)
XLA Modules:
  0.0 50.7 jit_solution(9798182299334272171)
XLA Ops:
  0.6 49.0 %unit.1 = (bf16[64,256]{1,0:T(8,128)(2,1)S(1)}, bf16[512,256]{1,0:T(8,128)(2,1)S(1)}, bf16[4,224,256]{2,1,0:T(8,128)(2,1)S(1)}) custom-call(bf16[512,256]{1,0:T(8,128)(2,1)} %bitcast.5, bf16[4,4,4,256]{3,2,1,0:T(4,128)(2,1)} %bitcast.6, bf16[28,32,256]{2,1,0:T(8,128)(2,1)} %w_hbm.1), custom_call_target="tpu_custom_call" | custom-call | tf_op jit(solution)/shard_map/unit/pallas_call | solution.py:425
  49.7 1.1 %finish.1 = (bf16[4,4,4,256]{3,2,1,0:T(4,128)(2,1)}, bf16[512,256]{1,0:T(8,128)(2,1)}, f32[4,224,256]{2,1,0:T(8,128)}) custom-call(bf16[64,256]{1,0:T(8,128)(2,1)S(1)} %get-tuple-element.9.out_v, bf16[512,256]{1,0:T(8,128)(2,1)S(1)} %get-tuple-element.10.ig_v, bf16[4,224,256]{2,1,0:T(8,128)(2,1)S(1)} %get-tuple-element.11.fin), custom_call_target="tpu_custom_call" | custom-call | tf_op jit(solution)/shard_map/finish/pallas_call | solution.py:440

commit v4 on v3

--- a/solution.py
+++ b/solution.py
@@ -56,11 +56,11 @@
            recv_x, recv_g, cols, gcols, wf, wcat, w27, dsilu, send_o, recv_o,
            send_i, recv_i, gsend, g1, s2, r2,
            in_sem, xs, xr, gs, gr, fs, os_, or_, is_, ir, s1s, s1r, s2s, s2r,
-           s3s, s3r, s4s, s4r, near, middle, across):
+           s3s, s3r, s4s, s4r, across):
     nq = 2 * nz
     taps_x = 28 // nx
     rows_q = s2.shape[1]
-    ring = s2.shape[0] // 2
+    ring = s2.shape[0]
     dp = lax.axis_index("dp")
     shard = lax.axis_index("shard")
     px = lax.rem(dp, nx)
@@ -85,18 +85,12 @@
         return at(lax.rem(pz + d + nz, nz), y, px, core)
 
     here = lax.rem(pz - lax.div(pz, IDLE + 1), nz) if ring < nz else pz
-    is_owner = pz != IDLE
-    mine = y_hi * ring + here
-
-    def owner(y_, n):
-        return at(n + lax.div(n, IDLE) if ring < nz else n, y_ * 4 + lax.rem(y, 4), px, core)
-
-    def order():
-        offsets = sorted(range(ring), key=lambda e: -min(e, ring - e))
-        for other_y in (1, 0):
-            for e in offsets:
-                y_ = 1 - y_hi if other_y else y_hi
-                yield not other_y and e == 0, y_, lax.rem(here + e, ring)
+    is_owner = (y_hi == 0) & (pz != IDLE) if ring < nz else y_hi == 0
+    near_first = sorted(range(ring), key=lambda e: min(e, ring - e))
+    order = [(e == 0, lax.rem(here + e, ring)) for e in near_first]
+
+    def owner(n):
+        return at(n + lax.div(n, IDLE) if ring < nz else n, lax.rem(y, 4), px, core)
 
     def piece(n):
         return pl.ds(pl.multiple_of(n * rows_q, 16), rows_q)
@@ -120,8 +114,7 @@
             peers.append(at(pz, y + d, px, c))
     peers += [at(pz, y + 2 * sign, px, core), at(pz, y + 2 * sign, px, 1 - core), at(pz, y - 2 * sign, px, core)]
     peers += [x_peer(d) for d in range(1, nx)]
-    if nz > 1:
-        peers += [z_peer(1), z_peer(-1)]
+    peers += [z_peer(d) for d in range(1, nz)] + [at(pz, y + 4, px, core)]
     barrier = pltpu.get_barrier_semaphore()
     for peer in peers:
         signal(barrier, peer)
@@ -161,9 +154,7 @@
             slot = 2 * k + core
             sends.append(copy(send_x.at[slice_of(to_chip(k), c)], recv_x.at[slot], xs.at[2 * k + e], xr.at[slot],
                               at(pz, to_chip(k), px, c)))
-    if nz > 1:
-        signal(near, z_peer(1))
-        signal(near, z_peer(-1))
+    signal(across, at(pz, y + 4, px, core))
     for send in sends:
         send.start()
     recv_x[core] = send_x[shard]
@@ -206,12 +197,25 @@
         sends.append(copy(recv_g.at[slot], recv_g.at[slot], fs.at[k], gr.at[slot], partner))
         sends[-1].start()
 
+    def returns(half):
+        rows = slice(half * 256, half * 256 + 256)
+        four = recv_g[4 * half:4 * half + 4].reshape(256, 256)
+        gcols[rows, 0:256] = four
+        for n in range(1, 8):
+            gcols[rows, n * 256:n * 256 + 256] = dot(shiftmt[n], four, NN).astype(BF16)
+        got = dot(gcols[rows, :], wcat[...], NT) * dsilu[rows, :]
+        direct = dot(four, w27[...], NT)
+        for n in range(4):
+            one = got[n * 64:n * 64 + 64, :]
+            slot = 4 * half + n
+            send_i[slot, :, 0:128] = (one[:, 0:128] + direct[n * 64:n * 64 + 64, :]).astype(BF16)
+            send_i[slot, :, 128:256] = one[:, 128:256].astype(BF16)
+        got = dot(cols[rows, :], wf[...], NN)
+        for n in range(4):
+            send_o[4 * half + n] = got[n * 64:n * 64 + 64, :].astype(BF16)
+
     for half in range(2):
         rows = slice(half * 256, half * 256 + 256)
-        if nz > 1 and half == 1:
-            pl.semaphore_wait(near, 2)
-            signal(middle, z_peer(2))
-            signal(middle, z_peer(-2))
         for k in (2 * half, 2 * half + 1):
             for e in (0, 1):
                 if k or e:
@@ -229,12 +233,10 @@
             if n == DIRECT:
                 moved = jnp.where(lane < 32, v, moved)
             cols[rows, first:first + width] = moved.astype(BF16)
-
-    for k in range(4):
-        arrived(recv_g, gr, 2 * k + 1 - core)
-    if nz > 1:
-        pl.semaphore_wait(middle, 2)
-    signal(across, at(pz, y + 4, px, core))
+        for k in (2 * half, 2 * half + 1):
+            arrived(recv_g, gr, 2 * k + 1 - core)
+        if half == 0:
+            returns(0)
 
     grads = recv_g[...].reshape(512, 256)
     for block in range(6):
@@ -253,32 +255,15 @@
                 place = (tap % taps_x) * 32
                 gsend[tap // taps_x, place:place + 32, :] = got[start:start + 32, :]
     step1 = []
-    for t, (_, y_, n) in enumerate(order()):
+    for t, (_, n) in enumerate(order[::-1]):
         for d in range(1, nx):
             other = lax.rem(px + d, nx)
             m = t * (nx - 1) + d - 1
-            part = piece(y_ * ring + n)
-            step1.append(copy(gsend.at[other, part], g1.at[d - 1, t], s1s.at[m], s1r.at[m], x_peer(d)))
+            step1.append(copy(gsend.at[other, piece(n)], g1.at[d - 1, t], s1s.at[m], s1r.at[m], x_peer(d)))
             step1[-1].start()
 
-    gcols[:, 0:256] = grads
-    for half in range(2):
-        rows = slice(half * 256, half * 256 + 256)
-        for n in range(1, 8):
-            gcols[rows, n * 256:n * 256 + 256] = dot(shiftmt[n], grads[rows, :], NN).astype(BF16)
-    for half in range(2):
-        rows = slice(half * 256, half * 256 + 256)
-        got = dot(gcols[rows, :], wcat[...], NT) * dsilu[rows, :]
-        direct = dot(grads[rows, :], w27[...], NT)
-        for n in range(4):
-            one = got[n * 64:n * 64 + 64, :]
-            slot = 4 * half + n
-            send_i[slot, :, 0:128] = (one[:, 0:128] + direct[n * 64:n * 64 + 64, :]).astype(BF16)
-            send_i[slot, :, 128:256] = one[:, 128:256].astype(BF16)
-        got = dot(cols[rows, :], wf[...], NN)
-        for n in range(4):
-            send_o[4 * half + n] = got[n * 64:n * 64 + 64, :].astype(BF16)
-    home = []
+    returns(1)
+    home, home_o = [], []
     for k in (3, 1, 2, 0):
         for e in (0, 1):
             if k == 0 and e == 0:
@@ -289,46 +274,37 @@
             dev = at(pz, chip, px, s)
             n = 2 * k + e
             home.append(copy(send_i.at[slot], recv_i.at[shard], is_.at[n], ir.at[shard], dev))
-            home.append(copy(send_o.at[slot], recv_o.at[shard], os_.at[n], or_.at[shard], dev))
-    pl.semaphore_wait(across, 1)
-    step2 = []
-    for t, (own, y_, n) in enumerate(order()):
-        for d in range(1, nx):
-            step1[t * (nx - 1) + d - 1].wait()
-        part = y_ * ring + n
-        total = gsend[px, piece(part), :].astype(F32)
-        for d in range(1, nx):
-            total = total + g1[d - 1, t].astype(F32)
-        s2[part] = total.astype(BF16)
-        send = copy(s2.at[part], r2.at[q], s2s.at[t], s2r.at[q], owner(y_, n))
-        if not own:
-            send.start()
-            step2.append(send)
-        elif ring < nz:
-            pl.when(pz == IDLE)(send.start)
-            last2 = send
-    r2[q] = s2[mine]
-
+            home_o.append(copy(send_o.at[slot], recv_o.at[shard], os_.at[n], or_.at[shard], dev))
     for send in home:
         send.start()
     recv_i[shard] = send_i[core]
     recv_o[shard] = send_o[core]
 
-    def for_owners(body):
-        if ring < nz:
-            pl.when(is_owner)(body)
+    pl.semaphore_wait(across, 1)
+    step2 = []
+    for t, (own, n) in enumerate(order[::-1]):
+        for d in range(1, nx):
+            step1[t * (nx - 1) + d - 1].wait()
+        total = gsend[px, piece(n), :].astype(F32)
+        for d in range(1, nx):
+            total = total + g1[d - 1, t].astype(F32)
+        s2[n] = total.astype(BF16)
+        step2.append(copy(s2.at[n], r2.at[q], s2s.at[t], s2r.at[q], owner(n)))
+        if own:
+            pl.when(jnp.logical_not(is_owner))(step2[-1].start)
         else:
-            body()
-
-    part = piece(mine)
-    step3 = [copy(fin.at[px, part], fin.at[px, part], s3s.at[t], s3r.at[q], owner(y_, n))
-             for t, (own, y_, n) in enumerate(order()) if not own]
-    if ring < nz:
-        for n, y_ in enumerate((1 - y_hi, y_hi)):
-            step3.append(copy(fin.at[px, part], fin.at[px, part], s3s.at[2 * ring + n], s3r.at[q],
-                              at(IDLE, y_ * 4 + lax.rem(y, 4), px, core)))
-
-    @for_owners
+            step2[-1].start()
+    r2[q] = s2[here]
+
+    part = piece(here)
+    step3 = []
+    for y_ in (0, 1):
+        for e in sorted(range(nz), key=lambda e: -min(e, nz - e)):
+            if y_ or e:
+                step3.append(copy(fin.at[px, part], fin.at[px, part], s3s.at[len(step3)], s3r.at[here],
+                                  at(lax.rem(pz + e, nz), y_ * 4 + lax.rem(y, 4), px, core)))
+
+    @pl.when(is_owner)
     def _():
         for d in range(1, nq):
             other = lax.rem(q + d, nq)
@@ -337,19 +313,18 @@
         for send in step3:
             send.start()
 
+    for send in home_o:
+        send.start()
     step4 = []
-    places = list(order())[::-1]
-    for t, (own, y_, n) in enumerate(places):
-        theirs = piece(y_ * ring + n)
-        sender = y_ * nz + (n + lax.div(n, IDLE) if ring < nz else n)
-        come = copy(fin.at[px, theirs], fin.at[px, theirs], s3s.at[0], s3r.at[sender], partner)
-        if not own:
+    for t, (own, n) in enumerate(order):
+        come = copy(fin.at[px, piece(n)], fin.at[px, piece(n)], s3s.at[0], s3r.at[n], partner)
+        if own:
+            pl.when(jnp.logical_not(is_owner))(come.wait_recv)
+        else:
             come.wait_recv()
-        elif ring < nz:
-            pl.when(pz == IDLE)(come.wait_recv)
         for d in range(1, nx):
             m = t * (nx - 1) + d - 1
-            step4.append(copy(fin.at[px, theirs], fin.at[px, theirs], s4s.at[m], s4r.at[m], x_peer(d)))
+            step4.append(copy(fin.at[px, piece(n)], fin.at[px, piece(n)], s4s.at[m], s4r.at[m], x_peer(d)))
             step4[-1].start()
 
     for e in range(1, 8):
@@ -365,18 +340,16 @@
         natural = sorted_x[:, b * 32:b * 32 + 32, :].reshape(256, 256).astype(BF16)
         ig_v[b * 256:b * 256 + 256, :] = dot(sortmt[...], natural, NN).astype(BF16)
 
-    for t, (own, y_, n) in enumerate(places):
-        theirs = piece(y_ * ring + n)
+    for t, (_, n) in enumerate(order):
         for d in range(1, nx):
             m = t * (nx - 1) + d - 1
             other = lax.rem(px + nx - d, nx)
-            copy(fin.at[other, theirs], fin.at[other, theirs], s4s.at[m], s4r.at[m], x_peer(d)).wait_recv()
-    for send in sends + home + step2 + step4:
+            copy(fin.at[other, piece(n)], fin.at[other, piece(n)], s4s.at[m], s4r.at[m], x_peer(d)).wait_recv()
+    for send in sends + home + home_o + step2[:-1] + step4:
         send.wait_send()
-    if ring < nz:
-        pl.when(pz == IDLE)(last2.wait_send)
-
-    @for_owners
+    pl.when(jnp.logical_not(is_owner))(step2[-1].wait_send)
+
+    @pl.when(is_owner)
     def _():
         for send in step3:
             send.wait_send()
@@ -399,13 +372,13 @@
 
 def shards(nx, nz, inputs, cotangent, weights):
     nq = 2 * nz
-    owners = 14 if nz == 8 else nq
+    owners = 7 if nz == 8 else nz
     rows_x = 28 // nx * 32
     rows_q = rows_x // owners
     dma = pltpu.SemaphoreType.DMA
     sems = [dma((n,)) for n in (3, 8, 8, 4, 8, 4, 8, 8, 8, 8)]
     sems += [dma((max(n, 1),)) for n in (owners * (nx - 1), owners * (nx - 1), nq, nq, nq, nq, owners * (nx - 1), owners * (nx - 1))]
-    sems += [pltpu.SemaphoreType.REGULAR] * 3
+    sems += [pltpu.SemaphoreType.REGULAR]
     vm = pltpu.VMEM
     scratch = [
         vm((512, 256), BF16), vm((4, 4, 4, 256), BF16), vm((64, 256), BF16), vm((28, 32, 256), BF16),

time: 50.9 us -> 54.3 us (1.067)
  the two profiles are of different devices: /device:TPU:1 before, /device:TPU:48 now
where the time goes in v4:
time: 54.3 us; the launch traced here: 54.1 us
  Pallas kernels  53.5 us (99%)
  between operations  0.64 us (1%)
    pallas_call x1, Pallas kernels, shards(): pl.pallas_call(functools.partial(kernel, nx, nz), out_shape=(jax.ShapeDty...  52.4 us

profile of v4, /device:TPU:48, one launch (start us, length us, event | category | flops | bytes accessed | tf_op | source)
XLA Modules:
  0.0 54.1 jit_solution(1218802922728153360)
XLA Ops:
  0.6 52.4 %unit.1 = (bf16[64,256]{1,0:T(8,128)(2,1)S(1)}, bf16[512,256]{1,0:T(8,128)(2,1)S(1)}, bf16[4,224,256]{2,1,0:T(8,128)(2,1)S(1)}) custom-call(bf16[512,256]{1,0:T(8,128)(2,1)} %bitcast.5, bf16[4,4,4,256]{3,2,1,0:T(4,128)(2,1)} %bitcast.6, bf16[28,32,256]{2,1,0:T(8,128)(2,1)} %w_hbm.1), custom_call_target="tpu_custom_call" | custom-call | tf_op jit(solution)/shard_map/unit/pallas_call | solution.py:398
  53.1 1.1 %finish.1 = (bf16[4,4,4,256]{3,2,1,0:T(4,128)(2,1)}, bf16[512,256]{1,0:T(8,128)(2,1)}, f32[4,224,256]{2,1,0:T(8,128)}) custom-call(bf16[64,256]{1,0:T(8,128)(2,1)S(1)} %get-tuple-element.9.out_v, bf16[512,256]{1,0:T(8,128)(2,1)S(1)} %get-tuple-element.10.ig_v, bf16[4,224,256]{2,1,0:T(8,128)(2,1)S(1)} %get-tuple-element.11.fin), custom_call_target="tpu_custom_call" | custom-call | tf_op jit(solution)/shard_map/finish/pallas_call | solution.py:413

commit v5 on v3

--- a/solution.py
+++ b/solution.py
@@ -56,7 +56,7 @@
            recv_x, recv_g, cols, gcols, wf, wcat, w27, dsilu, send_o, recv_o,
            send_i, recv_i, gsend, g1, s2, r2,
            in_sem, xs, xr, gs, gr, fs, os_, or_, is_, ir, s1s, s1r, s2s, s2r,
-           s3s, s3r, s4s, s4r, near, middle, across):
+           s3s, s3r, s4s, s4r, across):
     nq = 2 * nz
     taps_x = 28 // nx
     rows_q = s2.shape[1]
@@ -120,8 +120,7 @@
             peers.append(at(pz, y + d, px, c))
     peers += [at(pz, y + 2 * sign, px, core), at(pz, y + 2 * sign, px, 1 - core), at(pz, y - 2 * sign, px, core)]
     peers += [x_peer(d) for d in range(1, nx)]
-    if nz > 1:
-        peers += [z_peer(1), z_peer(-1)]
+    peers += [z_peer(d) for d in range(1, nz)] + [at(pz, y + 4, px, core)]
     barrier = pltpu.get_barrier_semaphore()
     for peer in peers:
         signal(barrier, peer)
@@ -161,9 +160,7 @@
             slot = 2 * k + core
             sends.append(copy(send_x.at[slice_of(to_chip(k), c)], recv_x.at[slot], xs.at[2 * k + e], xr.at[slot],
                               at(pz, to_chip(k), px, c)))
-    if nz > 1:
-        signal(near, z_peer(1))
-        signal(near, z_peer(-1))
+    signal(across, at(pz, y + 4, px, core))
     for send in sends:
         send.start()
     recv_x[core] = send_x[shard]
@@ -208,10 +205,6 @@
 
     for half in range(2):
         rows = slice(half * 256, half * 256 + 256)
-        if nz > 1 and half == 1:
-            pl.semaphore_wait(near, 2)
-            signal(middle, z_peer(2))
-            signal(middle, z_peer(-2))
         for k in (2 * half, 2 * half + 1):
             for e in (0, 1):
                 if k or e:
@@ -232,9 +225,6 @@
 
     for k in range(4):
         arrived(recv_g, gr, 2 * k + 1 - core)
-    if nz > 1:
-        pl.semaphore_wait(middle, 2)
-    signal(across, at(pz, y + 4, px, core))
 
     grads = recv_g[...].reshape(512, 256)
     for block in range(6):
@@ -309,8 +299,6 @@
             last2 = send
     r2[q] = s2[mine]
 
-    for send in home:
-        send.start()
     recv_i[shard] = send_i[core]
     recv_o[shard] = send_o[core]
 
@@ -337,6 +325,8 @@
         for send in step3:
             send.start()
 
+    for send in home:
+        send.start()
     step4 = []
     places = list(order())[::-1]
     for t, (own, y_, n) in enumerate(places):
@@ -405,7 +395,7 @@
     dma = pltpu.SemaphoreType.DMA
     sems = [dma((n,)) for n in (3, 8, 8, 4, 8, 4, 8, 8, 8, 8)]
     sems += [dma((max(n, 1),)) for n in (owners * (nx - 1), owners * (nx - 1), nq, nq, nq, nq, owners * (nx - 1), owners * (nx - 1))]
-    sems += [pltpu.SemaphoreType.REGULAR] * 3
+    sems += [pltpu.SemaphoreType.REGULAR]
     vm = pltpu.VMEM
     scratch = [
         vm((512, 256), BF16), vm((4, 4, 4, 256), BF16), vm((64, 256), BF16), vm((28, 32, 256), BF16),

time: 50.9 us -> 48.8 us (0.959)
  Pallas kernels: 50.1 us -> 48.1 us
    pallas_call x1, Pallas kernels: 49 us -> 47 us  [shards(): pl.pallas_call(functools.partial(kernel, nx, nz), out_shape=(jax.ShapeDty...]
where the time goes in v5:
time: 48.8 us; the launch traced here: 48.7 us
  Pallas kernels  48.1 us (99%)
  between operations  0.64 us (1%)
    pallas_call x1, Pallas kernels, shards(): pl.pallas_call(functools.partial(kernel, nx, nz), out_shape=(jax.ShapeDty...  47 us
    pallas_call x1, Pallas kernels, shards(): pl.pallas_call(finish, out_shape=(jax.ShapeDtypeStruct((4, 4, 4, 256), BF...  1.06 us

profile of v5, /device:TPU:1, one launch (start us, length us, event | category | flops | bytes accessed | tf_op | source)
XLA Modules:
  0.0 48.7 jit_solution(241136409876271266)
XLA Ops:
  0.6 47.0 %unit.1 = (bf16[64,256]{1,0:T(8,128)(2,1)S(1)}, bf16[512,256]{1,0:T(8,128)(2,1)S(1)}, bf16[4,224,256]{2,1,0:T(8,128)(2,1)S(1)}) custom-call(bf16[512,256]{1,0:T(8,128)(2,1)} %bitcast.5, bf16[4,4,4,256]{3,2,1,0:T(4,128)(2,1)} %bitcast.6, bf16[28,32,256]{2,1,0:T(8,128)(2,1)} %w_hbm.1), custom_call_target="tpu_custom_call" | custom-call | tf_op jit(solution)/shard_map/unit/pallas_call | solution.py:415
  47.6 1.1 %finish.1 = (bf16[4,4,4,256]{3,2,1,0:T(4,128)(2,1)}, bf16[512,256]{1,0:T(8,128)(2,1)}, f32[4,224,256]{2,1,0:T(8,128)}) custom-call(bf16[64,256]{1,0:T(8,128)(2,1)S(1)} %get-tuple-element.9.out_v, bf16[512,256]{1,0:T(8,128)(2,1)S(1)} %get-tuple-element.10.ig_v, bf16[4,224,256]{2,1,0:T(8,128)(2,1)S(1)} %get-tuple-element.11.fin), custom_call_target="tpu_custom_call" | custom-call | tf_op jit(solution)/shard_map/finish/pallas_call | solution.py:430

commit v6 on v5

--- a/solution.py
+++ b/solution.py
@@ -53,7 +53,7 @@
 
 def kernel(nx, nz, x_hbm, g_hbm, w_hbm, out_v, ig_v, fin,
            x_in, g_raw, g_in, w_in, sortm, sortmt, shiftm, shiftmt, sorted_x, send_x,
-           recv_x, recv_g, cols, gcols, wf, wcat, w27, dsilu, send_o, recv_o,
+           recv_x, recv_g, cols, gcols, wf, wcat, w27, dsilu, acc, send_o, recv_o,
            send_i, recv_i, gsend, g1, s2, r2,
            in_sem, xs, xr, gs, gr, fs, os_, or_, is_, ir, s1s, s1r, s2s, s2r,
            s3s, s3r, s4s, s4r, across):
@@ -152,7 +152,7 @@
         slot = 2 * k + core
         sends.append(copy(g_in, recv_g.at[slot], gs.at[k], gr.at[slot], at(pz, to_chip(k), px, core)))
     sends.append(copy(g_in, recv_g.at[core], gs.at[0], gr.at[core], partner))
-    for k in (3, 1, 2, 0):
+    for k in (0, 1, 3, 2):
         for e in (0, 1):
             if k == 0 and e == 0:
                 continue
@@ -222,13 +222,18 @@
             if n == DIRECT:
                 moved = jnp.where(lane < 32, v, moved)
             cols[rows, first:first + width] = moved.astype(BF16)
-
-    for k in range(4):
-        arrived(recv_g, gr, 2 * k + 1 - core)
+        for k in (2 * half, 2 * half + 1):
+            arrived(recv_g, gr, 2 * k + 1 - core)
+        if half == 0:
+            four = recv_g[0:4].reshape(256, 256)
+            for block in range(6):
+                acc[block * 256:block * 256 + 256, :] = dot(cols[0:256, block * 256:block * 256 + 256], four, TN)
+
 
     grads = recv_g[...].reshape(512, 256)
     for block in range(6):
-        got = dot(cols[:, block * 256:block * 256 + 256], grads, TN).astype(BF16)
+        got = dot(cols[256:, block * 256:block * 256 + 256], grads[256:], TN)
+        got = (got + acc[block * 256:block * 256 + 256, :]).astype(BF16)
         for n in range(8):
             first, width = lane_of(n)
             if first // 256 != block:
@@ -404,7 +409,7 @@
         vm((8, 64, 256), BF16), vm((8, 64, 256), BF16),
         vm((512, 1536), BF16), vm((512, 2048), BF16),
         vm((1536, 256), BF16), vm((256, 2048), BF16), vm((128, 256), BF16),
-        vm((512, 256), F32),
+        vm((512, 256), F32), vm((1536, 256), F32),
         vm((8, 64, 256), BF16), vm((8, 64, 256), BF16),
         vm((8, 64, 256), BF16), vm((8, 64, 256), BF16),
         vm((nx, rows_x, 256), BF16), vm((max(nx - 1, 1), owners, rows_q, 256), BF16),

time: 48.8 us -> 48.6 us (level)
  no operation moved by 1% of the time
where the time goes in v6:
time: 48.6 us; the launch traced here: 48.5 us
  Pallas kernels  47.8 us (98%)
  between operations  0.64 us (1%)
    pallas_call x1, Pallas kernels, shards(): pl.pallas_call(functools.partial(kernel, nx, nz), out_shape=(jax.ShapeDty...  46.8 us
    pallas_call x1, Pallas kernels, shards(): pl.pallas_call(finish, out_shape=(jax.ShapeDtypeStruct((4, 4, 4, 256), BF...  1.06 us

profile of v6, /device:TPU:1, one launch (start us, length us, event | category | flops | bytes accessed | tf_op | source)
XLA Modules:
  0.0 48.5 jit_solution(7032534116380945105)
XLA Ops:
  0.6 46.8 %unit.1 = (bf16[64,256]{1,0:T(8,128)(2,1)S(1)}, bf16[512,256]{1,0:T(8,128)(2,1)S(1)}, bf16[4,224,256]{2,1,0:T(8,128)(2,1)S(1)}) custom-call(bf16[512,256]{1,0:T(8,128)(2,1)} %bitcast.5, bf16[4,4,4,256]{3,2,1,0:T(4,128)(2,1)} %bitcast.6, bf16[28,32,256]{2,1,0:T(8,128)(2,1)} %w_hbm.1), custom_call_target="tpu_custom_call" | custom-call | tf_op jit(solution)/shard_map/unit/pallas_call | solution.py:420
  47.4 1.1 %finish.1 = (bf16[4,4,4,256]{3,2,1,0:T(4,128)(2,1)}, bf16[512,256]{1,0:T(8,128)(2,1)}, f32[4,224,256]{2,1,0:T(8,128)}) custom-call(bf16[64,256]{1,0:T(8,128)(2,1)S(1)} %get-tuple-element.9.out_v, bf16[512,256]{1,0:T(8,128)(2,1)S(1)} %get-tuple-element.10.ig_v, bf16[4,224,256]{2,1,0:T(8,128)(2,1)S(1)} %get-tuple-element.11.fin), custom_call_target="tpu_custom_call" | custom-call | tf_op jit(solution)/shard_map/finish/pallas_call | solution.py:435

commit v7 on v6

--- a/solution.py
+++ b/solution.py
@@ -289,7 +289,7 @@
     step2 = []
     for t, (own, y_, n) in enumerate(order()):
         for d in range(1, nx):
-            step1[t * (nx - 1) + d - 1].wait()
+            step1[t * (nx - 1) + d - 1].wait_recv()
         part = y_ * ring + n
         total = gsend[px, piece(part), :].astype(F32)
         for d in range(1, nx):
@@ -366,7 +366,7 @@
             m = t * (nx - 1) + d - 1
             other = lax.rem(px + nx - d, nx)
             copy(fin.at[other, theirs], fin.at[other, theirs], s4s.at[m], s4r.at[m], x_peer(d)).wait_recv()
-    for send in sends + home + step2 + step4:
+    for send in sends + step1 + home + step2 + step4:
         send.wait_send()
     if ring < nz:
         pl.when(pz == IDLE)(last2.wait_send)

time: 48.6 us -> 48.7 us (level)
  no operation moved by 1% of the time
where the time goes in v7:
time: 48.7 us; the launch traced here: 48.5 us
  Pallas kernels  47.9 us (98%)
  between operations  0.64 us (1%)
    pallas_call x1, Pallas kernels, shards(): pl.pallas_call(functools.partial(kernel, nx, nz), out_shape=(jax.ShapeDty...  46.8 us
    pallas_call x1, Pallas kernels, shards(): pl.pallas_call(finish, out_shape=(jax.ShapeDtypeStruct((4, 4, 4, 256), BF...  1.06 us

profile of v7, /device:TPU:1, one launch (start us, length us, event | category | flops | bytes accessed | tf_op | source)
XLA Modules:
  0.0 48.5 jit_solution(1994805737214923748)
XLA Ops:
  0.6 46.8 %unit.1 = (bf16[64,256]{1,0:T(8,128)(2,1)S(1)}, bf16[512,256]{1,0:T(8,128)(2,1)S(1)}, bf16[4,224,256]{2,1,0:T(8,128)(2,1)S(1)}) custom-call(bf16[512,256]{1,0:T(8,128)(2,1)} %bitcast.5, bf16[4,4,4,256]{3,2,1,0:T(4,128)(2,1)} %bitcast.6, bf16[28,32,256]{2,1,0:T(8,128)(2,1)} %w_hbm.1), custom_call_target="tpu_custom_call" | custom-call | tf_op jit(solution)/shard_map/unit/pallas_call | solution.py:420
  47.5 1.1 %finish.1 = (bf16[4,4,4,256]{3,2,1,0:T(4,128)(2,1)}, bf16[512,256]{1,0:T(8,128)(2,1)}, f32[4,224,256]{2,1,0:T(8,128)}) custom-call(bf16[64,256]{1,0:T(8,128)(2,1)S(1)} %get-tuple-element.9.out_v, bf16[512,256]{1,0:T(8,128)(2,1)S(1)} %get-tuple-element.10.ig_v, bf16[4,224,256]{2,1,0:T(8,128)(2,1)S(1)} %get-tuple-element.11.fin), custom_call_target="tpu_custom_call" | custom-call | tf_op jit(solution)/shard_map/finish/pallas_call | solution.py:435
